TPU v7x, 128 devices: a whole 4x4x4 slice. The times are simulated.
128 devices in a mesh: ctxa: 8 (over x, core), ctxb: 16 (over z, y).
Axes of the slice: x: 4, y: 4, z: 4, core: 2. Of those that a mesh axis runs over, the one named last changes fastest.
Arguments:
- tokens: bfloat16 [65536, 2048], P(('ctxa', 'ctxb')), may hold values from -6 to 6
- cotangent: bfloat16 [65536, 2048], P(('ctxa', 'ctxb')), may hold values from -6 to 6
- w_query: bfloat16 [2048, 1024], replicated, may hold values from -0.125 to 0.125
- w_key: bfloat16 [2048, 1024], replicated, may hold values from -0.125 to 0.125
- w_value: bfloat16 [2048, 1024], replicated, may hold values from -0.125 to 0.125
- w_out: bfloat16 [1024, 2048], replicated, may hold values from -0.125 to 0.125
Outputs:
- grad_tokens: bfloat16 [65536, 2048], P(('ctxa', 'ctxb'))
All inputs are finite; a program needn't handle non-finite values.
Results may differ from a plain program's by a relative error of at most 0.012.
Values may be sent and summed in bfloat16 or wider, within the bound.
A program may use at most 256 MiB of HBM per device.

v0:
```python
import math
import jax
import jax.numpy as jnp
from jax import lax
from jax.sharding import PartitionSpec as P

H = 8
DH = 128


def prefix(x, axis, join, neutral, backward):
    count = lax.axis_size(axis)
    place = lax.axis_index(axis)
    ahead = count - 1 - place if backward else place
    gathered = lax.all_gather(x.astype(jnp.bfloat16), axis)
    state = jnp.zeros_like(x) + jnp.asarray(neutral, x.dtype)

    def one(lap, state):
        source = count - 1 - lap if backward else lap
        return join(state, lax.dynamic_index_in_dim(gathered, source, 0, False).astype(x.dtype))

    return lax.fori_loop(0, ahead, one, state)


def project(left, weight):
    return jnp.dot(left, weight, preferred_element_type=jnp.float32).astype(jnp.bfloat16)


def add_states(earlier, later):
    return earlier + later


def regrouped_states(key_state, grad_state):
    key_group, grad_group = (
        lax.all_to_all(key_state[None], "ctxa", split_axis=1, concat_axis=0, tiled=True),
        lax.all_to_all(grad_state[None], "ctxa", split_axis=1, concat_axis=0, tiled=True),
    )
    key_total, grad_total = lax.psum((key_group, grad_group), "ctxb")
    key_row = prefix(key_group, "ctxb", add_states, jnp.zeros_like(key_group), False)
    grad_row = prefix(grad_group, "ctxb", add_states, jnp.zeros_like(grad_group), True)
    key_prior = jnp.cumsum(key_total, axis=0) - key_total + key_row
    grad_later = (
        jnp.sum(grad_total, axis=0, keepdims=True) - jnp.cumsum(grad_total, axis=0) + grad_row
    )
    key_prior = key_prior.astype(jnp.bfloat16)
    grad_later = grad_later.astype(jnp.bfloat16)
    returned = (
        lax.all_to_all(key_prior, "ctxa", split_axis=0, concat_axis=1, tiled=True),
        lax.all_to_all(grad_later, "ctxa", split_axis=0, concat_axis=1, tiled=True),
    )
    return (returned[0][0], returned[1][0])


def shards(tokens, cotangent, w_query, w_key, w_value, w_out):
    rows = tokens.shape[0]
    factor = 1.0 / math.sqrt(DH * rows * lax.axis_size("ctxa") * lax.axis_size("ctxb"))
    query = project(tokens, w_query).reshape(rows, H, DH)
    keys = project(tokens, w_key).reshape(rows, H, DH)
    values = project(tokens, w_value).reshape(rows, H, DH)
    grad_out = lax.dot_general(
        cotangent, w_out, (((1,), (1,)), ((), ())), preferred_element_type=jnp.float32
    )
    grad_out = grad_out.astype(jnp.bfloat16).reshape(rows, H, DH)
    key_state = jnp.einsum("rhi,rhj->hij", keys, values, preferred_element_type=jnp.float32)
    grad_state = jnp.einsum("rhi,rhj->hij", query, grad_out, preferred_element_type=jnp.float32)
    prior, later = regrouped_states(key_state, grad_state)
    index = jnp.arange(rows)
    causal = (index[:, None] >= index[None, :])[None]
    attend = jnp.where(
        causal, jnp.einsum("thi,shi->hts", query, keys, preferred_element_type=jnp.float32), 0.0
    ).astype(jnp.bfloat16)
    probe = jnp.where(
        causal,
        jnp.einsum("thj,shj->hts", grad_out, values, preferred_element_type=jnp.float32),
        0.0,
    ).astype(jnp.bfloat16)
    grad_query = jnp.einsum("hts,shi->thi", probe, keys, preferred_element_type=jnp.float32)
    grad_query = grad_query + jnp.einsum(
        "thj,hij->thi", grad_out, prior, preferred_element_type=jnp.float32
    )
    grad_key = jnp.einsum("hts,thi->shi", probe, query, preferred_element_type=jnp.float32)
    grad_key = grad_key + jnp.einsum(
        "shj,hij->shi", values, later, preferred_element_type=jnp.float32
    )
    grad_value = jnp.einsum("hts,thj->shj", attend, grad_out, preferred_element_type=jnp.float32)
    grad_value = grad_value + jnp.einsum(
        "shi,hij->shj", keys, later, preferred_element_type=jnp.float32
    )

    def finish(partial_grad):
        return (factor * partial_grad).astype(jnp.bfloat16).reshape(rows, H * DH)

    total = jnp.dot(finish(grad_query), w_query.T, preferred_element_type=jnp.float32)
    total = total + jnp.dot(finish(grad_key), w_key.T, preferred_element_type=jnp.float32)
    total = total + jnp.dot(finish(grad_value), w_value.T, preferred_element_type=jnp.float32)
    return total.astype(jnp.bfloat16)


def solution(mesh):
    placed = (P(("ctxa", "ctxb"), None), P(("ctxa", "ctxb"), None), P(), P(), P(), P())
    return jax.shard_map(
        shards, mesh=mesh, in_specs=placed, out_specs=P(("ctxa", "ctxb"), None), check_vma=False
    )
```

profile of v0, /device:TPU:1, one launch (start us, length us, event | category | flops | bytes accessed | tf_op | source)
XLA Modules:
  0.0 311.3 jit_solution(6295105417670766009)
XLA Ops:
  6.5 1.6 copy-done
  8.1 4.8 %fusion.5 = bf16[64,8,8,128]{3,2,1,0:T(8,128)(2,1)S(1)} fusion(bf16[512,2048]{1,0:T(8,128)(2,1)S(1)} %copy-done, bf16[2048,1024]{1,0:T(8,128)(2,1)} %param.13), kind=kOutput, calls=%fused_computation.16 | convolution fusion | flops 2148007936 | bytes 7340032 | tf_op jit(solution)/shard_map/dot_general | solution.py:26
  12.9 2.4 fusion.6
  16.3 1.4 convolution_bitcast_fusion.1
  17.7 5.8 %all-to-all-start = ((f32[1,8,128,128]{3,2,0,1:T(8,128)}), f32[1,8,128,128]{3,2,0,1:T(8,128)}, u32[]{:S(2)}, u32[]{:S(2)}) async-start(f32[1,8,128,128]{3,2,0,1:T(8,128)} %convolution_bitcast_fusion.1), calls=%async_computation | async-start | bytes 1048576 | tf_op jit(solution)/shard_map/all_to_all | solution.py:35
  23.5 5.6 %fusion.7 = bf16[64,8,8,128]{3,2,1,0:T(8,128)(2,1)} fusion(bf16[512,2048]{1,0:T(8,128)(2,1)S(1)} %copy-done, bf16[2048,1024]{1,0:T(8,128)(2,1)} %param.12), kind=kOutput, calls=%fused_computation.18 | convolution fusion | flops 2148007936 | bytes 7340032 | tf_op jit(solution)/shard_map/dot_general | solution.py:26
  29.1 3.3 %convolution_convert_fusion.2 = bf16[512,1024]{1,0:T(8,128)(2,1)} fusion(bf16[512,2048]{1,0:T(8,128)(2,1)S(1)} %copy-done.14, bf16[1024,2048]{1,0:T(8,128)(2,1)S(1)} %copy-done.9), kind=kOutput, calls=%fused_computation.14 | convolution fusion | flops 2148007936 | bytes 7340032 | tf_op jit(solution)/shard_map/dot_general | solution.py:60
  32.4 1.5 copy.49
  34.0 2.9 convolution_bitcast_fusion
  36.9 4.8 %all-to-all-start.2 = ((f32[1,8,128,128]{3,2,0,1:T(8,128)}), f32[1,8,128,128]{3,2,0,1:T(8,128)}, u32[]{:S(2)}, u32[]{:S(2)}) async-start(f32[1,8,128,128]{3,2,0,1:T(8,128)} %convolution_bitcast_fusion), calls=%async_computation.2 | async-start | bytes 1048576 | tf_op jit(solution)/shard_map/all_to_all | solution.py:36
  41.7 1.8 convert_bitcast_fusion.1
  43.5 7.7 %all-to-all-done.2 = f32[1,8,128,128]{3,2,0,1:T(8,128)} async-done(((f32[1,8,128,128]{3,2,0,1:T(8,128)}), f32[1,8,128,128]{3,2,0,1:T(8,128)}, u32[]{:S(2)}, u32[]{:S(2)}) %all-to-all-start.2) | async-done | bytes 524320 | tf_op jit(solution)/shard_map/all_to_all | solution.py:36
  51.1 1.8 convert_bitcast_fusion
  55.2 2.7 select_convert_fusion.1
  57.9 2.1 fusion.15
  60.1 2.9 fusion.25
  62.9 4.9 %fusion = f32[8,128,512]{2,1,0:T(8,128)} fusion(bf16[512,8,128]{0,2,1:T(8,128)(2,1)S(1)} %bitcast.111, pred[512,512]{1,0:T(8,128)(4,1)S(1)} %iota_compare_fusion, bf16[64,8,8,128]{3,2,1,0:T(8,128)(2,1)} %fusion.7, bf16[64,8,8,128]{3,2,1,0:T(8,128)(2,1)} %copy-done.2), kind=kOutput, calls=%fused_computation.4 | convolution fusion | flops 1077936128 | bytes 5505024 | tf_op jit(solution)/shard_map/hts,thj->shj/dot_general | solution.py:85
  67.8 76.2 %all-reduce.3.cloned.1.call-done = (f32[8,1,128,128]{3,2,0,1:T(8,128)}, f32[8,1,128,128]{3,2,0,1:T(8,128)}) async-done(((f32[8,1,128,128]{3,2,0,1:T(8,128)}, f32[8,1,128,128]{3,2,0,1:T(8,128)}), (f32[8,1,128,128]{3,2,0,1:T(8,128)}, f32[8,1,128,128]{3,2,0,1:T(8,128)})) %all-reduce.3.cloned.1.call-update) | async-done | bytes 1048592 | tf_op jit(solution)/shard_map/psum | solution.py:38
  144.0 1.1 reduce_sum.9
  145.1 53.2 %all-gather.5.cloned.1.call-done = bf16[16,8,128,128]{3,2,1,0:T(8,128)(2,1)} async-done(((bf16[1,8,128,128]{3,2,1,0:T(8,128)(2,1)}), bf16[16,8,128,128]{3,2,1,0:T(8,128)(2,1)}) %all-gather.5.cloned.1.call-update) | async-done | bytes 4194320 | tf_op jit(solution)/shard_map/all_gather | solution.py:15
  198.4 53.2 %all-gather.7.cloned.1.call-done = bf16[16,8,128,128]{3,2,1,0:T(8,128)(2,1)} async-done(((bf16[1,8,128,128]{3,2,1,0:T(8,128)(2,1)}), bf16[16,8,128,128]{3,2,1,0:T(8,128)(2,1)}) %all-gather.7.cloned.1.call-update) | async-done | bytes 4194320 | tf_op jit(solution)/shard_map/all_gather | solution.py:15
  251.6 16.4 %while.23 = (s32[]{:T(128)}, f32[8,1,128,128]{3,2,1,0:T(8,128)S(1)}, s32[]{:T(128)}, bf16[16,8,1,128,128]{4,3,1,2,0:T(8,128)(2,1)}, s32[]{:T(128)}, /*index=5*/s32[]{:T(128)}, s32[]{:T(128)}, s32[]{:T(128)}) while((s32[]{:T(128)}, f32[8,1,128,128]{3,2,1,0:T(8,128)S(1)}, s32[]{:T(128)}, bf16[16,8,1,128,128]{4,3,1,2,0:T(8,128)(2,1)}, s32[]{:T(128)}, ...), condition=%wide.region_8.9_spmd, body=%wide.region_7.8_spmd.sunk | while | flops 262150 | bytes 1310863 | solution.py:22
  251.7 1.1 convert_add_fusion.5
  252.8 1.1 convert_add_fusion.5
  253.9 1.1 convert_add_fusion.5
  254.9 1.1 convert_add_fusion.5
  256.0 1.1 convert_add_fusion.5
  257.1 1.1 convert_add_fusion.5
  258.2 1.1 convert_add_fusion.5
  259.3 1.1 convert_add_fusion.5
  260.4 1.1 convert_add_fusion.5
  261.5 1.1 convert_add_fusion.5
  262.6 1.1 convert_add_fusion.5
  263.7 1.1 convert_add_fusion.5
  264.8 1.1 convert_add_fusion.5
  265.9 1.1 convert_add_fusion.5
  267.0 1.1 convert_add_fusion.5
  268.0 2.0 fusion.11
  270.0 5.1 %all-to-all-start.1 = ((bf16[8,1,128,128]{3,2,1,0:T(8,128)(2,1)}), bf16[8,1,128,128]{3,2,1,0:T(8,128)(2,1)S(1)}, u32[]{:S(2)}, u32[]{:S(2)}) async-start(bf16[8,1,128,128]{3,2,1,0:T(8,128)(2,1)} %fusion.11), calls=%async_computation.1 | async-start | bytes 524288 | tf_op jit(solution)/shard_map/all_to_all | solution.py:48
  275.1 1.8 fusion.13
  276.9 4.7 %all-to-all-done.1 = bf16[8,1,128,128]{3,2,1,0:T(8,128)(2,1)S(1)} async-done(((bf16[8,1,128,128]{3,2,1,0:T(8,128)(2,1)}), bf16[8,1,128,128]{3,2,1,0:T(8,128)(2,1)S(1)}, u32[]{:S(2)}, u32[]{:S(2)}) %all-to-all-start.1) | async-done | bytes 262176 | tf_op jit(solution)/shard_map/all_to_all | solution.py:48
  281.6 4.4 %all-to-all-start.3 = ((bf16[8,1,128,128]{3,2,1,0:T(8,128)(2,1)}), bf16[8,1,128,128]{3,2,1,0:T(8,128)(2,1)S(1)}, u32[]{:S(2)}, u32[]{:S(2)}) async-start(bf16[8,1,128,128]{3,2,1,0:T(8,128)(2,1)} %fusion.13), calls=%async_computation.3 | async-start | bytes 524288 | tf_op jit(solution)/shard_map/all_to_all | solution.py:49
  285.9 2.5 multiply_convert_fusion.2
  289.1 4.3 %fusion.44 = f32[512,2048]{1,0:T(8,128)} fusion(bf16[512,1024]{0,1:T(8,128)(2,1)S(1)} %bitcast.114, bf16[2048,1024]{1,0:T(8,128)(2,1)S(1)} %copy-done.10), kind=kOutput, calls=%fused_computation.58 | convolution fusion | flops 2147483648 | bytes 9437184 | tf_op jit(solution)/shard_map/dot_general | solution.py:93
  293.4 2.2 multiply_convert_fusion.1
  296.2 2.4 fusion.45
  299.4 1.6 copy-done.13
  301.0 3.7 %add_convert_fusion = bf16[512,2048]{1,0:T(8,128)(2,1)} fusion(f32[512,2048]{1,0:T(8,128)S(1)} %copy-done.15, f32[512,2048]{1,0:T(8,128)S(1)} %fusion.45, bf16[512,1024]{0,1:T(8,128)(2,1)S(1)} %bitcast.113, bf16[2048,1024]{1,0:T(8,128)(2,1)S(1)} %copy-done.13), kind=kOutput, calls=%fused_computation.5 | convolution fusion | flops 2150629376 | bytes 15728640 | tf_op jit(solution)/shard_map/dot_general | solution.py:95
  (43 shorter events, 5.3 us)
Async XLA Ops:
  6.5 1.6 copy-start
  6.5 6.4 %copy-start.12 = (bf16[2048,1024]{1,0:T(8,128)(2,1)S(1)}, bf16[2048,1024]{1,0:T(8,128)(2,1)}, u32[]{:S(2)}) copy-start(bf16[2048,1024]{1,0:T(8,128)(2,1)} %param.14) | copy-start | bytes 12582916
  12.9 2.4 copy-start.2
  15.3 1.0 copy-start.7
  17.7 19.2 %all-to-all-start = ((f32[1,8,128,128]{3,2,0,1:T(8,128)}), f32[1,8,128,128]{3,2,0,1:T(8,128)}, u32[]{:S(2)}, u32[]{:S(2)}) async-start(f32[1,8,128,128]{3,2,0,1:T(8,128)} %convolution_bitcast_fusion.1), calls=%async_computation | async-start | bytes 1048576 | tf_op jit(solution)/shard_map/all_to_all | solution.py:35
  23.5 5.6 %copy-start.9 = (bf16[1024,2048]{1,0:T(8,128)(2,1)S(1)}, bf16[1024,2048]{1,0:T(8,128)(2,1)}, u32[]{:S(2)}) copy-start(bf16[1024,2048]{1,0:T(8,128)(2,1)} %param.15) | copy-start | bytes 12582916
  23.5 5.6 %copy-start.14 = (bf16[512,2048]{1,0:T(8,128)(2,1)S(1)}, bf16[512,2048]{1,0:T(8,128)(2,1)}, u32[]{:S(2)}) copy-start(bf16[512,2048]{1,0:T(8,128)(2,1)} %param.11) | copy-start | bytes 6291460
  33.9 29.0 %copy-start.1 = (bf16[512,1024]{0,1:T(8,128)(2,1)}, bf16[512,1024]{0,1:T(8,128)(2,1)S(1)}, u32[]{:S(2)}) copy-start(bf16[512,1024]{0,1:T(8,128)(2,1)S(1)} %copy.49) | copy-start | bytes 3145732
  36.9 14.3 %all-to-all-start.2 = ((f32[1,8,128,128]{3,2,0,1:T(8,128)}), f32[1,8,128,128]{3,2,0,1:T(8,128)}, u32[]{:S(2)}, u32[]{:S(2)}) async-start(f32[1,8,128,128]{3,2,0,1:T(8,128)} %convolution_bitcast_fusion), calls=%async_computation.2 | async-start | bytes 1048576 | tf_op jit(solution)/shard_map/all_to_all | solution.py:36
  52.9 91.1 %all-reduce.3.cloned.1.call-start = ((), (), s32[]{:S(2)}) async-start(), calls=%async_computation.6 | async-start | bytes 2097152 | tf_op jit(solution)/shard_map/psum | solution.py:38
  53.6 144.7 %all-gather.5.cloned.1.call-start = ((), (), s32[]{:S(2)}) async-start(), calls=%async_computation.4 | async-start | bytes 4456448 | tf_op jit(solution)/shard_map/all_gather | solution.py:15
  54.4 197.2 %all-gather.7.cloned.1.call-start = ((), (), s32[]{:S(2)}) async-start(), calls=%async_computation.5 | async-start | bytes 4456448 | tf_op jit(solution)/shard_map/all_gather | solution.py:15
  55.1 2.8 copy-start.5
  57.9 2.2 copy-start.3
  270.0 11.6 %all-to-all-start.1 = ((bf16[8,1,128,128]{3,2,1,0:T(8,128)(2,1)}), bf16[8,1,128,128]{3,2,1,0:T(8,128)(2,1)S(1)}, u32[]{:S(2)}, u32[]{:S(2)}) async-start(bf16[8,1,128,128]{3,2,1,0:T(8,128)(2,1)} %fusion.11), calls=%async_computation.1 | async-start | bytes 524288 | tf_op jit(solution)/shard_map/all_to_all | solution.py:48
  281.6 11.8 %all-to-all-start.3 = ((bf16[8,1,128,128]{3,2,1,0:T(8,128)(2,1)}), bf16[8,1,128,128]{3,2,1,0:T(8,128)(2,1)S(1)}, u32[]{:S(2)}, u32[]{:S(2)}) async-start(bf16[8,1,128,128]{3,2,1,0:T(8,128)(2,1)} %fusion.13), calls=%async_computation.3 | async-start | bytes 524288 | tf_op jit(solution)/shard_map/all_to_all | solution.py:49
  285.9 3.1 %copy-start.10 = (bf16[2048,1024]{1,0:T(8,128)(2,1)S(1)}, bf16[2048,1024]{1,0:T(8,128)(2,1)}, u32[]{:S(2)}) copy-start(bf16[2048,1024]{1,0:T(8,128)(2,1)} %param.12) | copy-start | bytes 12582916
  289.1 4.3 %copy-start.8 = (bf16[64,8,8,128]{3,2,1,0:T(8,128)(2,1)S(1)}, bf16[64,8,8,128]{3,2,1,0:T(8,128)(2,1)}, u32[]{:S(2)}) copy-start(bf16[64,8,8,128]{3,2,1,0:T(8,128)(2,1)} %copy-done.7) | copy-start | bytes 3145732
  293.4 2.8 copy-start.11
  296.2 2.4 copy-start.4
  296.2 2.4 copy-start.6
  296.2 3.2 %copy-start.15 = (f32[512,2048]{1,0:T(8,128)S(1)}, f32[512,2048]{1,0:T(8,128)}, u32[]{:S(2)}) copy-start(f32[512,2048]{1,0:T(8,128)} %fusion.44) | copy-start | bytes 12582916
  298.6 2.4 copy-start.13
Sparse Core Ops, SparseCore 0:
  57.0 86.9 all-reduce.2
  146.2 52.1 all-gather.4
  200.5 51.0 all-gather.6
where the time goes:
time: 313 us; the launch traced here: 311 us
  waiting for transfers between devices  197 us (63%)
  matrix products  48.6 us (16%)
  other arithmetic  24.5 us (8%)
  starting transfers between devices  20.3 us (6%)
  between operations  13.3 us (4%)
  local copies, waits for them, and re-layouts  7.28 us (2%)
    all_gather x2, waiting for transfers between devices, prefix(): gathered = lax.all_gather(x.astype(jnp.bfloat16), axis)  106 us
    psum x1, waiting for transfers between devices, regrouped_states(): key_total, grad_total = lax.psum((key_group, grad_group), 'ctxb')  76.2 us
    add x15, other arithmetic, add_states(): return earlier + later  16 us
    dot_general x3, matrix products, project(): jnp.dot(left, weight, preferred_element_type=jnp.float32)  12.8 us
    all_to_all x1, waiting for transfers between devices, regrouped_states(): lax.all_to_all(grad_state[None], 'ctxa', split_axis=1, concat_axis=0, til...  7.67 us
  transfers between devices with their start and end apart: 7, of which 5 were waited for; matrix products, arithmetic and copies ran while one was open for 12% of the time, Pallas kernels for 0%

commit v1 on v0

--- a/solution.py
+++ b/solution.py
@@ -1,3 +1,4 @@
+import functools
 import math
 import jax
 import jax.numpy as jnp
@@ -6,6 +7,22 @@
 
 H = 8
 DH = 128
+
+
+def quotas_form(x_in, a_name):
+    back = jnp.concatenate(
+        lax.all_to_all(
+            jnp.stack(jnp.split(x_in, lax.axis_size(a_name), axis=1)),
+            axis_name=a_name,
+            split_axis=0,
+            concat_axis=0,
+        ),
+        axis=0,
+    )
+    return back
+
+
+attach_pairs_all = functools.partial(quotas_form, a_name="ctxa")
 
 
 def prefix(x, axis, join, neutral, backward):
@@ -33,7 +50,7 @@
 def regrouped_states(key_state, grad_state):
     key_group, grad_group = (
         lax.all_to_all(key_state[None], "ctxa", split_axis=1, concat_axis=0, tiled=True),
-        lax.all_to_all(grad_state[None], "ctxa", split_axis=1, concat_axis=0, tiled=True),
+        attach_pairs_all(grad_state[None]),
     )
     key_total, grad_total = lax.psum((key_group, grad_group), "ctxb")
     key_row = prefix(key_group, "ctxb", add_states, jnp.zeros_like(key_group), False)

time: 313 us -> 317 us (1.013)
  local copies, waits for them, and re-layouts: 7.28 us -> 12.4 us
    unnamed x32 -> x39, local copies, waits for them, and re-layouts: 5.72 us -> 10.2 us
  transfers between devices with their start and end apart: 7 -> 7, of which waited for: 5 -> 5; matrix products, arithmetic and copies ran while one was open for 12% -> 13% of each run, Pallas kernels for 0% -> 0%
where the time goes in v1:
time: 317 us; the launch traced here: 316 us
  waiting for transfers between devices  197 us (62%)
  matrix products  47.8 us (15%)
  other arithmetic  24.5 us (8%)
  starting transfers between devices  20.3 us (6%)
  between operations  13.3 us (4%)
  local copies, waits for them, and re-layouts  12.4 us (4%)
    all_gather x2, waiting for transfers between devices, prefix(): gathered = lax.all_gather(x.astype(jnp.bfloat16), axis)  106 us
    psum x1, waiting for transfers between devices, regrouped_states(): key_total, grad_total = lax.psum((key_group, grad_group), 'ctxb')  76.2 us
    add x15, other arithmetic, add_states(): return earlier + later  16 us
    dot_general x3, matrix products, project(): jnp.dot(left, weight, preferred_element_type=jnp.float32)  12.8 us
    unnamed x39, local copies, waits for them, and re-layouts  10.2 us
    all_to_all x1, waiting for transfers between devices, quotas_form(): lax.all_to_all(jnp.stack(jnp.split(x_in, lax.axis_size(a_name), axis=1)),...  7.67 us
  transfers between devices with their start and end apart: 7, of which 5 were waited for; matrix products, arithmetic and copies ran while one was open for 13% of the time, Pallas kernels for 0%

profile of v1, /device:TPU:1, one launch (start us, length us, event | category | flops | bytes accessed | tf_op | source)
XLA Modules:
  0.0 315.6 jit_solution(7136257142909681555)
XLA Ops:
  6.5 1.6 copy-done
  8.1 4.8 %fusion.5 = bf16[64,8,8,128]{3,2,1,0:T(8,128)(2,1)S(1)} fusion(bf16[512,2048]{1,0:T(8,128)(2,1)S(1)} %copy-done, bf16[2048,1024]{1,0:T(8,128)(2,1)} %param.13), kind=kOutput, calls=%fused_computation.16 | convolution fusion | flops 2148007936 | bytes 7340032 | tf_op jit(solution)/shard_map/dot_general | solution.py:43
  12.9 2.4 fusion.6
  16.3 1.4 convolution_bitcast_fusion.1
  17.7 5.8 %all-to-all-start = ((f32[1,8,128,128]{3,2,0,1:T(8,128)}), f32[1,8,128,128]{3,2,0,1:T(8,128)}, u32[]{:S(2)}, u32[]{:S(2)}) async-start(f32[1,8,128,128]{3,2,0,1:T(8,128)} %convolution_bitcast_fusion.1), calls=%async_computation | async-start | bytes 1048576 | tf_op jit(solution)/shard_map/all_to_all | solution.py:52
  23.5 5.6 %fusion.7 = bf16[64,8,8,128]{3,2,1,0:T(8,128)(2,1)} fusion(bf16[512,2048]{1,0:T(8,128)(2,1)S(1)} %copy-done, bf16[2048,1024]{1,0:T(8,128)(2,1)} %param.12), kind=kOutput, calls=%fused_computation.18 | convolution fusion | flops 2148007936 | bytes 7340032 | tf_op jit(solution)/shard_map/dot_general | solution.py:43
  29.1 3.3 %convolution_convert_fusion.2 = bf16[512,1024]{1,0:T(8,128)(2,1)} fusion(bf16[512,2048]{1,0:T(8,128)(2,1)S(1)} %copy-done.14, bf16[1024,2048]{1,0:T(8,128)(2,1)S(1)} %copy-done.9), kind=kOutput, calls=%fused_computation.14 | convolution fusion | flops 2148007936 | bytes 7340032 | tf_op jit(solution)/shard_map/dot_general | solution.py:77
  32.4 1.5 copy.47
  34.0 2.1 convolution_bitcast_fusion
  41.1 4.8 %all-to-all-start.2 = ((f32[8,1,1,128,128]{4,3,2,1,0:T(8,128)}), f32[8,1,1,128,128]{4,3,2,1,0:T(8,128)}, u32[]{:S(2)}, u32[]{:S(2)}) async-start(f32[8,1,1,128,128]{4,3,2,1,0:T(8,128)} %fusion.43), calls=%async_computation.2 | async-start | bytes 1048576 | tf_op jit(solution)/shard_map/all_to_all | solution.py:14
  46.0 1.8 convert_bitcast_fusion
  47.7 7.7 %all-to-all-done.2 = f32[8,1,1,128,128]{4,3,2,1,0:T(8,128)} async-done(((f32[8,1,1,128,128]{4,3,2,1,0:T(8,128)}), f32[8,1,1,128,128]{4,3,2,1,0:T(8,128)}, u32[]{:S(2)}, u32[]{:S(2)}) %all-to-all-start.2) | async-done | bytes 524320 | tf_op jit(solution)/shard_map/all_to_all | solution.py:14
  55.4 1.8 convert_element_type.116
  59.5 2.7 select_convert_fusion.1
  62.2 2.1 fusion.15
  64.4 2.9 fusion.25
  67.2 4.9 %fusion = f32[8,128,512]{2,1,0:T(8,128)} fusion(bf16[512,8,128]{0,2,1:T(8,128)(2,1)S(1)} %bitcast.139, pred[512,512]{1,0:T(8,128)(4,1)S(1)} %iota_compare_fusion, bf16[64,8,8,128]{3,2,1,0:T(8,128)(2,1)} %fusion.7, bf16[64,8,8,128]{3,2,1,0:T(8,128)(2,1)} %copy-done.2), kind=kOutput, calls=%fused_computation.4 | convolution fusion | flops 1077936128 | bytes 5505024 | tf_op jit(solution)/shard_map/hts,thj->shj/dot_general | solution.py:102
  72.1 76.2 %all-reduce.3.cloned.1.call-done = (f32[8,1,128,128]{3,2,0,1:T(8,128)}, f32[8,1,128,128]{3,2,0,1:T(8,128)}) async-done(((f32[8,1,128,128]{3,2,0,1:T(8,128)}, f32[8,1,128,128]{3,2,0,1:T(8,128)}), (f32[8,1,128,128]{3,2,0,1:T(8,128)}, f32[8,1,128,128]{3,2,0,1:T(8,128)})) %all-reduce.3.cloned.1.call-update) | async-done | bytes 1048592 | tf_op jit(solution)/shard_map/psum | solution.py:55
  148.3 1.1 reduce_sum.9
  149.4 53.2 %all-gather.5.cloned.1.call-done = bf16[16,8,128,128]{3,2,1,0:T(8,128)(2,1)} async-done(((bf16[1,8,128,128]{3,2,1,0:T(8,128)(2,1)}), bf16[16,8,128,128]{3,2,1,0:T(8,128)(2,1)}) %all-gather.5.cloned.1.call-update) | async-done | bytes 4194320 | tf_op jit(solution)/shard_map/all_gather | solution.py:32
  202.7 53.2 %all-gather.7.cloned.1.call-done = bf16[128,1,1,128,128]{4,3,2,1,0:T(8,128)(2,1)} async-done(((bf16[8,1,1,128,128]{4,3,2,1,0:T(8,128)(2,1)}), bf16[128,1,1,128,128]{4,3,2,1,0:T(8,128)(2,1)}) %all-gather.7.cloned.1.call-update) | async-done | bytes 4194320 | tf_op jit(solution)/shard_map/all_gather | solution.py:32
  256.0 16.4 %while.23 = (s32[]{:T(128)}, f32[8,1,128,128]{3,2,1,0:T(8,128)S(1)}, s32[]{:T(128)}, bf16[16,8,1,128,128]{4,3,1,2,0:T(8,128)(2,1)}, s32[]{:T(128)}, /*index=5*/s32[]{:T(128)}, s32[]{:T(128)}, s32[]{:T(128)}) while((s32[]{:T(128)}, f32[8,1,128,128]{3,2,1,0:T(8,128)S(1)}, s32[]{:T(128)}, bf16[16,8,1,128,128]{4,3,1,2,0:T(8,128)(2,1)}, s32[]{:T(128)}, ...), condition=%wide.region_8.9_spmd, body=%wide.region_7.8_spmd.sunk | while | flops 262150 | bytes 1310863 | solution.py:39
  256.0 1.1 convert_add_fusion.5
  257.1 1.1 convert_add_fusion.5
  258.2 1.1 convert_add_fusion.5
  259.3 1.1 convert_add_fusion.5
  260.3 1.1 convert_add_fusion.5
  261.4 1.1 convert_add_fusion.5
  262.5 1.1 convert_add_fusion.5
  263.6 1.1 convert_add_fusion.5
  264.7 1.1 convert_add_fusion.5
  265.8 1.1 convert_add_fusion.5
  266.9 1.1 convert_add_fusion.5
  268.0 1.1 convert_add_fusion.5
  269.1 1.1 convert_add_fusion.5
  270.2 1.1 convert_add_fusion.5
  271.3 1.1 convert_add_fusion.5
  272.4 2.0 fusion.11
  274.3 5.1 %all-to-all-start.1 = ((bf16[8,1,128,128]{3,2,1,0:T(8,128)(2,1)}), bf16[8,1,128,128]{3,2,1,0:T(8,128)(2,1)S(1)}, u32[]{:S(2)}, u32[]{:S(2)}) async-start(bf16[8,1,128,128]{3,2,1,0:T(8,128)(2,1)} %fusion.11), calls=%async_computation.1 | async-start | bytes 524288 | tf_op jit(solution)/shard_map/all_to_all | solution.py:65
  279.4 1.8 fusion.13
  281.2 4.7 %all-to-all-done.1 = bf16[8,1,128,128]{3,2,1,0:T(8,128)(2,1)S(1)} async-done(((bf16[8,1,128,128]{3,2,1,0:T(8,128)(2,1)}), bf16[8,1,128,128]{3,2,1,0:T(8,128)(2,1)S(1)}, u32[]{:S(2)}, u32[]{:S(2)}) %all-to-all-start.1) | async-done | bytes 262176 | tf_op jit(solution)/shard_map/all_to_all | solution.py:65
  285.9 4.4 %all-to-all-start.3 = ((bf16[8,1,128,128]{3,2,1,0:T(8,128)(2,1)}), bf16[8,1,128,128]{3,2,1,0:T(8,128)(2,1)S(1)}, u32[]{:S(2)}, u32[]{:S(2)}) async-start(bf16[8,1,128,128]{3,2,1,0:T(8,128)(2,1)} %fusion.13), calls=%async_computation.3 | async-start | bytes 524288 | tf_op jit(solution)/shard_map/all_to_all | solution.py:66
  290.2 2.5 multiply_convert_fusion.2
  293.4 4.3 %fusion.52 = f32[512,2048]{1,0:T(8,128)} fusion(bf16[512,1024]{0,1:T(8,128)(2,1)S(1)} %bitcast.142, bf16[2048,1024]{1,0:T(8,128)(2,1)S(1)} %copy-done.10), kind=kOutput, calls=%fused_computation.73 | convolution fusion | flops 2147483648 | bytes 9437184 | tf_op jit(solution)/shard_map/dot_general | solution.py:110
  297.7 2.2 multiply_convert_fusion.1
  300.5 2.4 fusion.53
  303.7 1.6 copy-done.13
  305.3 3.7 %add_convert_fusion = bf16[512,2048]{1,0:T(8,128)(2,1)} fusion(f32[512,2048]{1,0:T(8,128)S(1)} %copy-done.15, f32[512,2048]{1,0:T(8,128)S(1)} %fusion.53, bf16[512,1024]{0,1:T(8,128)(2,1)S(1)} %bitcast.141, bf16[2048,1024]{1,0:T(8,128)(2,1)S(1)} %copy-done.13), kind=kOutput, calls=%fused_computation.5 | convolution fusion | flops 2150629376 | bytes 15728640 | tf_op jit(solution)/shard_map/dot_general | solution.py:112
  (51 shorter events, 10.4 us)
Async XLA Ops:
  6.5 1.6 copy-start
  6.5 6.4 %copy-start.12 = (bf16[2048,1024]{1,0:T(8,128)(2,1)S(1)}, bf16[2048,1024]{1,0:T(8,128)(2,1)}, u32[]{:S(2)}) copy-start(bf16[2048,1024]{1,0:T(8,128)(2,1)} %param.14) | copy-start | bytes 12582916
  12.9 2.4 copy-start.2
  15.3 1.0 copy-start.7
  17.7 23.5 %all-to-all-start = ((f32[1,8,128,128]{3,2,0,1:T(8,128)}), f32[1,8,128,128]{3,2,0,1:T(8,128)}, u32[]{:S(2)}, u32[]{:S(2)}) async-start(f32[1,8,128,128]{3,2,0,1:T(8,128)} %convolution_bitcast_fusion.1), calls=%async_computation | async-start | bytes 1048576 | tf_op jit(solution)/shard_map/all_to_all | solution.py:52
  23.5 5.6 %copy-start.9 = (bf16[1024,2048]{1,0:T(8,128)(2,1)S(1)}, bf16[1024,2048]{1,0:T(8,128)(2,1)}, u32[]{:S(2)}) copy-start(bf16[1024,2048]{1,0:T(8,128)(2,1)} %param.15) | copy-start | bytes 12582916
  23.5 5.6 %copy-start.14 = (bf16[512,2048]{1,0:T(8,128)(2,1)S(1)}, bf16[512,2048]{1,0:T(8,128)(2,1)}, u32[]{:S(2)}) copy-start(bf16[512,2048]{1,0:T(8,128)(2,1)} %param.11) | copy-start | bytes 6291460
  33.9 33.3 %copy-start.1 = (bf16[512,1024]{0,1:T(8,128)(2,1)}, bf16[512,1024]{0,1:T(8,128)(2,1)S(1)}, u32[]{:S(2)}) copy-start(bf16[512,1024]{0,1:T(8,128)(2,1)S(1)} %copy.47) | copy-start | bytes 3145732
  41.1 14.3 %all-to-all-start.2 = ((f32[8,1,1,128,128]{4,3,2,1,0:T(8,128)}), f32[8,1,1,128,128]{4,3,2,1,0:T(8,128)}, u32[]{:S(2)}, u32[]{:S(2)}) async-start(f32[8,1,1,128,128]{4,3,2,1,0:T(8,128)} %fusion.43), calls=%async_computation.2 | async-start | bytes 1048576 | tf_op jit(solution)/shard_map/all_to_all | solution.py:14
  57.2 91.1 %all-reduce.3.cloned.1.call-start = ((), (), s32[]{:S(2)}) async-start(), calls=%async_computation.6 | async-start | bytes 2097152 | tf_op jit(solution)/shard_map/psum | solution.py:55
  57.9 144.7 %all-gather.5.cloned.1.call-start = ((), (), s32[]{:S(2)}) async-start(), calls=%async_computation.4 | async-start | bytes 4456448 | tf_op jit(solution)/shard_map/all_gather | solution.py:32
  58.7 197.3 %all-gather.7.cloned.1.call-start = ((), (), s32[]{:S(2)}) async-start(), calls=%async_computation.5 | async-start | bytes 4456448 | tf_op jit(solution)/shard_map/all_gather | solution.py:32
  59.4 2.8 copy-start.5
  62.2 2.2 copy-start.3
  274.3 11.6 %all-to-all-start.1 = ((bf16[8,1,128,128]{3,2,1,0:T(8,128)(2,1)}), bf16[8,1,128,128]{3,2,1,0:T(8,128)(2,1)S(1)}, u32[]{:S(2)}, u32[]{:S(2)}) async-start(bf16[8,1,128,128]{3,2,1,0:T(8,128)(2,1)} %fusion.11), calls=%async_computation.1 | async-start | bytes 524288 | tf_op jit(solution)/shard_map/all_to_all | solution.py:65
  285.9 11.8 %all-to-all-start.3 = ((bf16[8,1,128,128]{3,2,1,0:T(8,128)(2,1)}), bf16[8,1,128,128]{3,2,1,0:T(8,128)(2,1)S(1)}, u32[]{:S(2)}, u32[]{:S(2)}) async-start(bf16[8,1,128,128]{3,2,1,0:T(8,128)(2,1)} %fusion.13), calls=%async_computation.3 | async-start | bytes 524288 | tf_op jit(solution)/shard_map/all_to_all | solution.py:66
  290.2 3.1 copy-start.10
  293.4 4.3 %copy-start.8 = (bf16[64,8,8,128]{3,2,1,0:T(8,128)(2,1)S(1)}, bf16[64,8,8,128]{3,2,1,0:T(8,128)(2,1)}, u32[]{:S(2)}) copy-start(bf16[64,8,8,128]{3,2,1,0:T(8,128)(2,1)} %copy-done.7) | copy-start | bytes 3145732
  297.7 2.8 copy-start.11
  300.5 2.4 copy-start.4
  300.5 2.4 copy-start.6
  300.5 3.2 copy-start.15
  302.9 2.4 copy-start.13
Sparse Core Ops, SparseCore 0:
  61.3 86.9 all-reduce.2
  150.5 52.1 all-gather.4
  204.8 51.0 all-gather.6
